TPU v7x, 32 devices: a whole 2x2x4 slice. The times are simulated.
32 devices in a mesh: row: 4 (over x, core), col: 8 (over z, y).
Axes of the slice: x: 2, y: 2, z: 4, core: 2. Of those that a mesh axis runs over, the one named last changes fastest.
Arguments:
- optical_field: float32 [2, 512, 4096], P(None, 'row', 'col'), may hold values from -6 to 6
- index_panels: bfloat16 [5, 512, 4096], P(None, ('row', 'col')), may hold values from -4 to 4
Outputs:
- propagated: float32 [2, 512, 4096], P(None, 'row', 'col')
All inputs are finite; a program needn't handle non-finite values.
Results may differ from a plain program's by a relative error of at most 0.0003.
Values may be sent and summed in bfloat16 or wider, within the bound.
A program may use at most 64 MiB of HBM per device.

v0:
```python
import jax
import jax.numpy as jnp
from jax import lax
from jax.sharding import PartitionSpec as P

STEPS = 2


diffraction = 0.15
phase_gain = 0.25


def with_halo(cells, sides, width):
    for axis, dim in sides:
        count = lax.axis_size(axis)
        head = lax.slice_in_dim(cells, 0, width, axis=dim)
        tail = lax.slice_in_dim(cells, cells.shape[dim] - width, cells.shape[dim], axis=dim)
        cells = jnp.concatenate(
            [
                lax.ppermute(tail, axis, [(i, (i + 1) % count) for i in range(count)]),
                cells,
                lax.ppermute(head, axis, [((i + 1) % count, i) for i in range(count)]),
            ],
            axis=dim,
        )
    return cells


def laplace(padded):
    centre = padded[:, 2:-2, 2:-2]
    along_y = 16.0 * (padded[:, 1:-3, 2:-2] + padded[:, 3:-1, 2:-2]) - (
        padded[:, :-4, 2:-2] + padded[:, 4:, 2:-2]
    )
    along_x = 16.0 * (padded[:, 2:-2, 1:-3] + padded[:, 2:-2, 3:-1]) - (
        padded[:, 2:-2, :-4] + padded[:, 2:-2, 4:]
    )
    return (along_y + along_x - 60.0 * centre) / 12.0


def slope(padded, plane):
    centre = padded[:, 2:-2, 2:-2]
    total = diffraction * laplace(padded) + phase_gain * plane.astype(jnp.float32) * centre
    return jnp.stack([-total[1], total[0]])


def section_slope(state, plane):
    padded = with_halo(state, (("row", 1), ("col", 2)), 2)
    return slope(padded, plane)


def local(optical_field, index_panels):
    planes_all = lax.all_to_all(index_panels, "col", split_axis=2, concat_axis=1, tiled=True)
    field = optical_field
    planes = None
    for step_index in range(STEPS):
        first = 2 * step_index
        planes = planes_all[first : first + 3]
        first_slope = section_slope(field, planes[0])
        second_slope = section_slope(field + 0.5 * first_slope, planes[1])
        third_slope = section_slope(field + 0.5 * second_slope, planes[1])
        fourth_slope = section_slope(field + third_slope, planes[2])
        field = field + (first_slope + 2.0 * second_slope + 2.0 * third_slope + fourth_slope) / 6.0
    return field


def solution(mesh):
    in_specs = (P(None, "row", "col"), P(None, ("row", "col"), None))
    out_specs = P(None, "row", "col")
    return jax.shard_map(local, mesh=mesh, in_specs=in_specs, out_specs=out_specs, check_vma=False)
```

profile of v0, /device:TPU:0, one launch (start us, length us, event | category | flops | bytes accessed | tf_op | source)
XLA Modules:
  0.0 162.4 jit_solution(11394870547222477419)
XLA Ops:
  0.0 8.1 %copy.10 = bf16[5,16,4096]{1,0,2:T(8,128)(2,1)} copy(bf16[5,16,4096]{2,1,0:T(8,128)(2,1)} %param.3) | data formatting | bytes 1310720 | tf_op args[1]
  8.1 9.1 %reshape.60 = bf16[8,2,20480]{2,1,0:T(2,128)(2,1)} reshape(bf16[4096,5,16]{2,1,0:T(8,128)(2,1)} %bitcast.10) | data formatting | bytes 1310720
  17.2 7.3 %all-to-all-start = ((bf16[8,2,20480]{2,1,0:T(2,128)(2,1)}), bf16[8,2,20480]{2,1,0:T(2,128)(2,1)S(1)}, u32[]{:S(2)}, u32[]{:S(2)}) async-start(bf16[8,2,20480]{2,1,0:T(2,128)(2,1)} %reshape.60), calls=%async_computation | async-start | bytes 1310720 | tf_op jit(solution)/shard_map/all_to_all | solution.py:52
  27.8 2.1 %collective-permute-start.2 = (f32[2,132,2]{2,1,0:T(8,128)S(1)}, f32[2,132,2]{2,1,0:T(8,128)S(1)}, u32[]{:S(2)}, u32[]{:S(2)}) collective-permute-start(f32[2,132,2]{2,1,0:T(8,128)S(1)} %get-tuple-element.40), channel_id=1, source_target_pairs={{0,1},{1,2},{2,3},{3,4},{4,5},{5,6},{6,7},{7,0},{8,9},{9,10},{10,1... | collective-permute-start | bytes 6344 | tf_op jit(solution)/shard_map/ppermute | solution.py:20
  29.8 2.8 %collective-permute-start.3 = (f32[2,132,2]{2,1,0:T(8,128)S(1)}, f32[2,132,2]{2,1,0:T(8,128)S(1)}, u32[]{:S(2)}, u32[]{:S(2)}) collective-permute-start(f32[2,132,2]{2,1,0:T(8,128)S(1)} %get-tuple-element.41), channel_id=1, source_target_pairs={{1,0},{2,1},{3,2},{4,3},{5,4},{6,5},{7,6},{0,7},{9,8},{10,9},{11,1... | collective-permute-start | bytes 6344 | tf_op jit(solution)/shard_map/ppermute | solution.py:22
  32.6 10.5 %collective-permute-done.2 = f32[2,132,2]{2,1,0:T(8,128)S(1)} collective-permute-done((f32[2,132,2]{2,1,0:T(8,128)S(1)}, f32[2,132,2]{2,1,0:T(8,128)S(1)}, u32[]{:S(2)}, u32[]{:S(2)}) %collective-permute-start.2) | collective-permute-done | bytes 2144 | tf_op jit(solution)/shard_map/ppermute | solution.py:20
  43.4 7.3 %reshape.61 = bf16[4096,5,16]{2,1,0:T(8,128)(2,1)} reshape(bf16[8,2,20480]{2,1,0:T(2,128)(2,1)S(1)} %all-to-all-done) | data formatting | bytes 1310720
  50.7 6.4 %copy.17 = bf16[5,16,8,512]{3,2,1,0:T(8,128)(2,1)S(1)} copy(bf16[5,16,8,512]{1,0,3,2:T(8,128)(2,1)} %bitcast.9) | data formatting | bytes 1310720 | tf_op jit(solution)/shard_map/all_to_all | solution.py:52
  61.5 2.8 %collective-permute-start.6 = (f32[2,132,2]{2,1,0:T(8,128)S(1)}, f32[2,132,2]{2,1,0:T(8,128)S(1)}, u32[]{:S(2)}, u32[]{:S(2)}) collective-permute-start(f32[2,132,2]{2,1,0:T(8,128)S(1)} %get-tuple-element.36), channel_id=1, source_target_pairs={{0,1},{1,2},{2,3},{3,4},{4,5},{5,6},{6,7},{7,0},{8,9},{9,10},{10,1... | collective-permute-start | bytes 6344 | tf_op jit(solution)/shard_map/ppermute | solution.py:20
  64.3 2.0 %collective-permute-start.7 = (f32[2,132,2]{2,1,0:T(8,128)S(1)}, f32[2,132,2]{2,1,0:T(8,128)S(1)}, u32[]{:S(2)}, u32[]{:S(2)}) collective-permute-start(f32[2,132,2]{2,1,0:T(8,128)S(1)} %get-tuple-element.37), channel_id=1, source_target_pairs={{1,0},{2,1},{3,2},{4,3},{5,4},{6,5},{7,6},{0,7},{9,8},{10,9},{11,1... | collective-permute-start | bytes 6344 | tf_op jit(solution)/shard_map/ppermute | solution.py:22
  66.5 4.4 %collective-permute-done.6 = f32[2,132,2]{2,1,0:T(8,128)S(1)} collective-permute-done((f32[2,132,2]{2,1,0:T(8,128)S(1)}, f32[2,132,2]{2,1,0:T(8,128)S(1)}, u32[]{:S(2)}, u32[]{:S(2)}) %collective-permute-start.6) | collective-permute-done | bytes 2144 | tf_op jit(solution)/shard_map/ppermute | solution.py:20
  70.8 2.9 %collective-permute-done.7 = f32[2,132,2]{2,1,0:T(8,128)S(1)} collective-permute-done((f32[2,132,2]{2,1,0:T(8,128)S(1)}, f32[2,132,2]{2,1,0:T(8,128)S(1)}, u32[]{:S(2)}, u32[]{:S(2)}) %collective-permute-start.7) | collective-permute-done | bytes 2144 | tf_op jit(solution)/shard_map/ppermute | solution.py:22
  78.2 4.7 %collective-permute-start.11 = (f32[2,132,2]{2,1,0:T(8,128)S(1)}, f32[2,132,2]{2,1,0:T(8,128)S(1)}, u32[]{:S(2)}, u32[]{:S(2)}) collective-permute-start(f32[2,132,2]{2,1,0:T(8,128)S(1)} %get-tuple-element.33), channel_id=1, source_target_pairs={{1,0},{2,1},{3,2},{4,3},{5,4},{6,5},{7,6},{0,7},{9,8},{10,9},{11,1... | collective-permute-start | bytes 6344 | tf_op jit(solution)/shard_map/ppermute | solution.py:22
  82.9 4.6 %collective-permute-done.10 = f32[2,132,2]{2,1,0:T(8,128)S(1)} collective-permute-done((f32[2,132,2]{2,1,0:T(8,128)S(1)}, f32[2,132,2]{2,1,0:T(8,128)S(1)}, u32[]{:S(2)}, u32[]{:S(2)}) %collective-permute-start.10) | collective-permute-done | bytes 2144 | tf_op jit(solution)/shard_map/ppermute | solution.py:20
  92.2 4.7 %collective-permute-start.15 = (f32[2,132,2]{2,1,0:T(8,128)S(1)}, f32[2,132,2]{2,1,0:T(8,128)S(1)}, u32[]{:S(2)}, u32[]{:S(2)}) collective-permute-start(f32[2,132,2]{2,1,0:T(8,128)S(1)} %get-tuple-element.29), channel_id=1, source_target_pairs={{1,0},{2,1},{3,2},{4,3},{5,4},{6,5},{7,6},{0,7},{9,8},{10,9},{11,1... | collective-permute-start | bytes 6344 | tf_op jit(solution)/shard_map/ppermute | solution.py:22
  97.1 4.2 %collective-permute-done.14 = f32[2,132,2]{2,1,0:T(8,128)S(1)} collective-permute-done((f32[2,132,2]{2,1,0:T(8,128)S(1)}, f32[2,132,2]{2,1,0:T(8,128)S(1)}, u32[]{:S(2)}, u32[]{:S(2)}) %collective-permute-start.14) | collective-permute-done | bytes 2144 | tf_op jit(solution)/shard_map/ppermute | solution.py:20
  105.9 5.1 %collective-permute-start.19 = (f32[2,132,2]{2,1,0:T(8,128)S(1)}, f32[2,132,2]{2,1,0:T(8,128)S(1)}, u32[]{:S(2)}, u32[]{:S(2)}) collective-permute-start(f32[2,132,2]{2,1,0:T(8,128)S(1)} %get-tuple-element.25), channel_id=1, source_target_pairs={{1,0},{2,1},{3,2},{4,3},{5,4},{6,5},{7,6},{0,7},{9,8},{10,9},{11,1... | collective-permute-start | bytes 6344 | tf_op jit(solution)/shard_map/ppermute | solution.py:22
  111.0 3.8 %collective-permute-done.18 = f32[2,132,2]{2,1,0:T(8,128)S(1)} collective-permute-done((f32[2,132,2]{2,1,0:T(8,128)S(1)}, f32[2,132,2]{2,1,0:T(8,128)S(1)}, u32[]{:S(2)}, u32[]{:S(2)}) %collective-permute-start.18) | collective-permute-done | bytes 2144 | tf_op jit(solution)/shard_map/ppermute | solution.py:20
  119.7 5.3 %collective-permute-start.23 = (f32[2,132,2]{2,1,0:T(8,128)S(1)}, f32[2,132,2]{2,1,0:T(8,128)S(1)}, u32[]{:S(2)}, u32[]{:S(2)}) collective-permute-start(f32[2,132,2]{2,1,0:T(8,128)S(1)} %get-tuple-element.21), channel_id=1, source_target_pairs={{1,0},{2,1},{3,2},{4,3},{5,4},{6,5},{7,6},{0,7},{9,8},{10,9},{11,1... | collective-permute-start | bytes 6344 | tf_op jit(solution)/shard_map/ppermute | solution.py:22
  125.1 3.9 %collective-permute-done.22 = f32[2,132,2]{2,1,0:T(8,128)S(1)} collective-permute-done((f32[2,132,2]{2,1,0:T(8,128)S(1)}, f32[2,132,2]{2,1,0:T(8,128)S(1)}, u32[]{:S(2)}, u32[]{:S(2)}) %collective-permute-start.22) | collective-permute-done | bytes 2144 | tf_op jit(solution)/shard_map/ppermute | solution.py:20
  134.7 4.5 %collective-permute-start.27 = (f32[2,132,2]{2,1,0:T(8,128)S(1)}, f32[2,132,2]{2,1,0:T(8,128)S(1)}, u32[]{:S(2)}, u32[]{:S(2)}) collective-permute-start(f32[2,132,2]{2,1,0:T(8,128)S(1)} %get-tuple-element.17), channel_id=1, source_target_pairs={{1,0},{2,1},{3,2},{4,3},{5,4},{6,5},{7,6},{0,7},{9,8},{10,9},{11,1... | collective-permute-start | bytes 6344 | tf_op jit(solution)/shard_map/ppermute | solution.py:22
  139.3 4.2 %collective-permute-done.26 = f32[2,132,2]{2,1,0:T(8,128)S(1)} collective-permute-done((f32[2,132,2]{2,1,0:T(8,128)S(1)}, f32[2,132,2]{2,1,0:T(8,128)S(1)}, u32[]{:S(2)}, u32[]{:S(2)}) %collective-permute-start.26) | collective-permute-done | bytes 2144 | tf_op jit(solution)/shard_map/ppermute | solution.py:20
  149.8 4.5 %collective-permute-start.31 = (f32[2,132,2]{2,1,0:T(8,128)S(1)}, f32[2,132,2]{2,1,0:T(8,128)S(1)}, u32[]{:S(2)}, u32[]{:S(2)}) collective-permute-start(f32[2,132,2]{2,1,0:T(8,128)S(1)} %get-tuple-element.13), channel_id=1, source_target_pairs={{1,0},{2,1},{3,2},{4,3},{5,4},{6,5},{7,6},{0,7},{9,8},{10,9},{11,1... | collective-permute-start | bytes 6344 | tf_op jit(solution)/shard_map/ppermute | solution.py:22
  154.5 4.0 %collective-permute-done.30 = f32[2,132,2]{2,1,0:T(8,128)S(1)} collective-permute-done((f32[2,132,2]{2,1,0:T(8,128)S(1)}, f32[2,132,2]{2,1,0:T(8,128)S(1)}, u32[]{:S(2)}, u32[]{:S(2)}) %collective-permute-start.30) | collective-permute-done | bytes 2144 | tf_op jit(solution)/shard_map/ppermute | solution.py:20
  (104 shorter events, 42.9 us)
Async XLA Ops:
  17.2 26.2 %all-to-all-start = ((bf16[8,2,20480]{2,1,0:T(2,128)(2,1)}), bf16[8,2,20480]{2,1,0:T(2,128)(2,1)S(1)}, u32[]{:S(2)}, u32[]{:S(2)}) async-start(bf16[8,2,20480]{2,1,0:T(2,128)(2,1)} %reshape.60), calls=%async_computation | async-start | bytes 1310720 | tf_op jit(solution)/shard_map/all_to_all | solution.py:52
  24.5 3.1 %collective-permute-start = (f32[2,2,512]{2,1,0:T(2,128)S(1)}, f32[2,2,512]{2,1,0:T(2,128)S(1)}, u32[]{:S(2)}, u32[]{:S(2)}) collective-permute-start(f32[2,2,512]{2,1,0:T(2,128)S(1)} %get-tuple-element.73), channel_id=1, source_target_pairs={{0,8},{8,16},{16,24},{24,0},{1,9},{9,17},{17,25},{25,1},{2,10},{10... | collective-permute-start | bytes 24584 | tf_op jit(solution)/shard_map/ppermute | solution.py:20
  27.8 15.4 %collective-permute-start.2 = (f32[2,132,2]{2,1,0:T(8,128)S(1)}, f32[2,132,2]{2,1,0:T(8,128)S(1)}, u32[]{:S(2)}, u32[]{:S(2)}) collective-permute-start(f32[2,132,2]{2,1,0:T(8,128)S(1)} %get-tuple-element.40), channel_id=1, source_target_pairs={{0,1},{1,2},{2,3},{3,4},{4,5},{5,6},{6,7},{7,0},{8,9},{9,10},{10,1... | collective-permute-start | bytes 6344 | tf_op jit(solution)/shard_map/ppermute | solution.py:20
  29.8 13.3 %collective-permute-start.3 = (f32[2,132,2]{2,1,0:T(8,128)S(1)}, f32[2,132,2]{2,1,0:T(8,128)S(1)}, u32[]{:S(2)}, u32[]{:S(2)}) collective-permute-start(f32[2,132,2]{2,1,0:T(8,128)S(1)} %get-tuple-element.41), channel_id=1, source_target_pairs={{1,0},{2,1},{3,2},{4,3},{5,4},{6,5},{7,6},{0,7},{9,8},{10,9},{11,1... | collective-permute-start | bytes 6344 | tf_op jit(solution)/shard_map/ppermute | solution.py:22
  58.2 3.1 %collective-permute-start.4 = (f32[2,2,512]{2,1,0:T(2,128)S(1)}, f32[2,2,512]{2,1,0:T(2,128)S(1)}, u32[]{:S(2)}, u32[]{:S(2)}) collective-permute-start(f32[2,2,512]{2,1,0:T(2,128)S(1)} %get-tuple-element.68), channel_id=1, source_target_pairs={{0,8},{8,16},{16,24},{24,0},{1,9},{9,17},{17,25},{25,1},{2,10},{10... | collective-permute-start | bytes 24584 | tf_op jit(solution)/shard_map/ppermute | solution.py:20
  61.5 9.3 %collective-permute-start.6 = (f32[2,132,2]{2,1,0:T(8,128)S(1)}, f32[2,132,2]{2,1,0:T(8,128)S(1)}, u32[]{:S(2)}, u32[]{:S(2)}) collective-permute-start(f32[2,132,2]{2,1,0:T(8,128)S(1)} %get-tuple-element.36), channel_id=1, source_target_pairs={{0,1},{1,2},{2,3},{3,4},{4,5},{5,6},{6,7},{7,0},{8,9},{9,10},{10,1... | collective-permute-start | bytes 6344 | tf_op jit(solution)/shard_map/ppermute | solution.py:20
  64.3 9.4 %collective-permute-start.7 = (f32[2,132,2]{2,1,0:T(8,128)S(1)}, f32[2,132,2]{2,1,0:T(8,128)S(1)}, u32[]{:S(2)}, u32[]{:S(2)}) collective-permute-start(f32[2,132,2]{2,1,0:T(8,128)S(1)} %get-tuple-element.37), channel_id=1, source_target_pairs={{1,0},{2,1},{3,2},{4,3},{5,4},{6,5},{7,6},{0,7},{9,8},{10,9},{11,1... | collective-permute-start | bytes 6344 | tf_op jit(solution)/shard_map/ppermute | solution.py:22
  74.9 3.1 %collective-permute-start.8 = (f32[2,2,512]{2,1,0:T(2,128)S(1)}, f32[2,2,512]{2,1,0:T(2,128)S(1)}, u32[]{:S(2)}, u32[]{:S(2)}) collective-permute-start(f32[2,2,512]{2,1,0:T(2,128)S(1)} %get-tuple-element.64), channel_id=1, source_target_pairs={{0,8},{8,16},{16,24},{24,0},{1,9},{9,17},{17,25},{25,1},{2,10},{10... | collective-permute-start | bytes 24584 | tf_op jit(solution)/shard_map/ppermute | solution.py:20
  78.2 9.3 %collective-permute-start.10 = (f32[2,132,2]{2,1,0:T(8,128)S(1)}, f32[2,132,2]{2,1,0:T(8,128)S(1)}, u32[]{:S(2)}, u32[]{:S(2)}) collective-permute-start(f32[2,132,2]{2,1,0:T(8,128)S(1)} %get-tuple-element.32), channel_id=1, source_target_pairs={{0,1},{1,2},{2,3},{3,4},{4,5},{5,6},{6,7},{7,0},{8,9},{9,10},{10,1... | collective-permute-start | bytes 6344 | tf_op jit(solution)/shard_map/ppermute | solution.py:20
  78.2 9.5 %collective-permute-start.11 = (f32[2,132,2]{2,1,0:T(8,128)S(1)}, f32[2,132,2]{2,1,0:T(8,128)S(1)}, u32[]{:S(2)}, u32[]{:S(2)}) collective-permute-start(f32[2,132,2]{2,1,0:T(8,128)S(1)} %get-tuple-element.33), channel_id=1, source_target_pairs={{1,0},{2,1},{3,2},{4,3},{5,4},{6,5},{7,6},{0,7},{9,8},{10,9},{11,1... | collective-permute-start | bytes 6344 | tf_op jit(solution)/shard_map/ppermute | solution.py:22
  88.8 3.1 %collective-permute-start.12 = (f32[2,2,512]{2,1,0:T(2,128)S(1)}, f32[2,2,512]{2,1,0:T(2,128)S(1)}, u32[]{:S(2)}, u32[]{:S(2)}) collective-permute-start(f32[2,2,512]{2,1,0:T(2,128)S(1)} %get-tuple-element.60), channel_id=1, source_target_pairs={{0,8},{8,16},{16,24},{24,0},{1,9},{9,17},{17,25},{25,1},{2,10},{10... | collective-permute-start | bytes 24584 | tf_op jit(solution)/shard_map/ppermute | solution.py:20
  92.1 9.1 %collective-permute-start.14 = (f32[2,132,2]{2,1,0:T(8,128)S(1)}, f32[2,132,2]{2,1,0:T(8,128)S(1)}, u32[]{:S(2)}, u32[]{:S(2)}) collective-permute-start(f32[2,132,2]{2,1,0:T(8,128)S(1)} %get-tuple-element.28), channel_id=1, source_target_pairs={{0,1},{1,2},{2,3},{3,4},{4,5},{5,6},{6,7},{7,0},{8,9},{9,10},{10,1... | collective-permute-start | bytes 6344 | tf_op jit(solution)/shard_map/ppermute | solution.py:20
  92.2 9.0 %collective-permute-start.15 = (f32[2,132,2]{2,1,0:T(8,128)S(1)}, f32[2,132,2]{2,1,0:T(8,128)S(1)}, u32[]{:S(2)}, u32[]{:S(2)}) collective-permute-start(f32[2,132,2]{2,1,0:T(8,128)S(1)} %get-tuple-element.29), channel_id=1, source_target_pairs={{1,0},{2,1},{3,2},{4,3},{5,4},{6,5},{7,6},{0,7},{9,8},{10,9},{11,1... | collective-permute-start | bytes 6344 | tf_op jit(solution)/shard_map/ppermute | solution.py:22
  102.5 3.1 %collective-permute-start.16 = (f32[2,2,512]{2,1,0:T(2,128)S(1)}, f32[2,2,512]{2,1,0:T(2,128)S(1)}, u32[]{:S(2)}, u32[]{:S(2)}) collective-permute-start(f32[2,2,512]{2,1,0:T(2,128)S(1)} %get-tuple-element.56), channel_id=1, source_target_pairs={{0,8},{8,16},{16,24},{24,0},{1,9},{9,17},{17,25},{25,1},{2,10},{10... | collective-permute-start | bytes 24584 | tf_op jit(solution)/shard_map/ppermute | solution.py:20
  105.8 9.0 %collective-permute-start.18 = (f32[2,132,2]{2,1,0:T(8,128)S(1)}, f32[2,132,2]{2,1,0:T(8,128)S(1)}, u32[]{:S(2)}, u32[]{:S(2)}) collective-permute-start(f32[2,132,2]{2,1,0:T(8,128)S(1)} %get-tuple-element.24), channel_id=1, source_target_pairs={{0,1},{1,2},{2,3},{3,4},{4,5},{5,6},{6,7},{7,0},{8,9},{9,10},{10,1... | collective-permute-start | bytes 6344 | tf_op jit(solution)/shard_map/ppermute | solution.py:20
  105.9 9.1 %collective-permute-start.19 = (f32[2,132,2]{2,1,0:T(8,128)S(1)}, f32[2,132,2]{2,1,0:T(8,128)S(1)}, u32[]{:S(2)}, u32[]{:S(2)}) collective-permute-start(f32[2,132,2]{2,1,0:T(8,128)S(1)} %get-tuple-element.25), channel_id=1, source_target_pairs={{1,0},{2,1},{3,2},{4,3},{5,4},{6,5},{7,6},{0,7},{9,8},{10,9},{11,1... | collective-permute-start | bytes 6344 | tf_op jit(solution)/shard_map/ppermute | solution.py:22
  116.3 3.1 %collective-permute-start.20 = (f32[2,2,512]{2,1,0:T(2,128)S(1)}, f32[2,2,512]{2,1,0:T(2,128)S(1)}, u32[]{:S(2)}, u32[]{:S(2)}) collective-permute-start(f32[2,2,512]{2,1,0:T(2,128)S(1)} %get-tuple-element.52), channel_id=1, source_target_pairs={{0,8},{8,16},{16,24},{24,0},{1,9},{9,17},{17,25},{25,1},{2,10},{10... | collective-permute-start | bytes 24584 | tf_op jit(solution)/shard_map/ppermute | solution.py:20
  119.6 9.4 %collective-permute-start.22 = (f32[2,132,2]{2,1,0:T(8,128)S(1)}, f32[2,132,2]{2,1,0:T(8,128)S(1)}, u32[]{:S(2)}, u32[]{:S(2)}) collective-permute-start(f32[2,132,2]{2,1,0:T(8,128)S(1)} %get-tuple-element.20), channel_id=1, source_target_pairs={{0,1},{1,2},{2,3},{3,4},{4,5},{5,6},{6,7},{7,0},{8,9},{9,10},{10,1... | collective-permute-start | bytes 6344 | tf_op jit(solution)/shard_map/ppermute | solution.py:20
  119.7 10.2 %collective-permute-start.23 = (f32[2,132,2]{2,1,0:T(8,128)S(1)}, f32[2,132,2]{2,1,0:T(8,128)S(1)}, u32[]{:S(2)}, u32[]{:S(2)}) collective-permute-start(f32[2,132,2]{2,1,0:T(8,128)S(1)} %get-tuple-element.21), channel_id=1, source_target_pairs={{1,0},{2,1},{3,2},{4,3},{5,4},{6,5},{7,6},{0,7},{9,8},{10,9},{11,1... | collective-permute-start | bytes 6344 | tf_op jit(solution)/shard_map/ppermute | solution.py:22
  134.5 9.0 %collective-permute-start.26 = (f32[2,132,2]{2,1,0:T(8,128)S(1)}, f32[2,132,2]{2,1,0:T(8,128)S(1)}, u32[]{:S(2)}, u32[]{:S(2)}) collective-permute-start(f32[2,132,2]{2,1,0:T(8,128)S(1)} %get-tuple-element.16), channel_id=1, source_target_pairs={{0,1},{1,2},{2,3},{3,4},{4,5},{5,6},{6,7},{7,0},{8,9},{9,10},{10,1... | collective-permute-start | bytes 6344 | tf_op jit(solution)/shard_map/ppermute | solution.py:20
  134.7 10.2 %collective-permute-start.27 = (f32[2,132,2]{2,1,0:T(8,128)S(1)}, f32[2,132,2]{2,1,0:T(8,128)S(1)}, u32[]{:S(2)}, u32[]{:S(2)}) collective-permute-start(f32[2,132,2]{2,1,0:T(8,128)S(1)} %get-tuple-element.17), channel_id=1, source_target_pairs={{1,0},{2,1},{3,2},{4,3},{5,4},{6,5},{7,6},{0,7},{9,8},{10,9},{11,1... | collective-permute-start | bytes 6344 | tf_op jit(solution)/shard_map/ppermute | solution.py:22
  146.3 3.1 %collective-permute-start.28 = (f32[2,2,512]{2,1,0:T(2,128)S(1)}, f32[2,2,512]{2,1,0:T(2,128)S(1)}, u32[]{:S(2)}, u32[]{:S(2)}) collective-permute-start(f32[2,2,512]{2,1,0:T(2,128)S(1)} %get-tuple-element.44), channel_id=1, source_target_pairs={{0,8},{8,16},{16,24},{24,0},{1,9},{9,17},{17,25},{25,1},{2,10},{10... | collective-permute-start | bytes 24584 | tf_op jit(solution)/shard_map/ppermute | solution.py:20
  149.6 9.0 %collective-permute-start.30 = (f32[2,132,2]{2,1,0:T(8,128)S(1)}, f32[2,132,2]{2,1,0:T(8,128)S(1)}, u32[]{:S(2)}, u32[]{:S(2)}) collective-permute-start(f32[2,132,2]{2,1,0:T(8,128)S(1)} %get-tuple-element.12), channel_id=1, source_target_pairs={{0,1},{1,2},{2,3},{3,4},{4,5},{5,6},{6,7},{7,0},{8,9},{9,10},{10,1... | collective-permute-start | bytes 6344 | tf_op jit(solution)/shard_map/ppermute | solution.py:20
  149.8 10.2 %collective-permute-start.31 = (f32[2,132,2]{2,1,0:T(8,128)S(1)}, f32[2,132,2]{2,1,0:T(8,128)S(1)}, u32[]{:S(2)}, u32[]{:S(2)}) collective-permute-start(f32[2,132,2]{2,1,0:T(8,128)S(1)} %get-tuple-element.13), channel_id=1, source_target_pairs={{1,0},{2,1},{3,2},{4,3},{5,4},{6,5},{7,6},{0,7},{9,8},{10,9},{11,1... | collective-permute-start | bytes 6344 | tf_op jit(solution)/shard_map/ppermute | solution.py:22
  (10 other events, 51.2 us)
where the time goes:
time: 163 us; the launch traced here: 162 us
  starting transfers between devices  60.8 us (37%)
  waiting for transfers between devices  57.7 us (35%)
  local copies, waits for them, and re-layouts  31.8 us (20%)
  other arithmetic  11.7 us (7%)
    ppermute x16, waiting for transfers between devices, with_halo(): lax.ppermute(tail, axis, [(i, (i + 1) % count) for i in range(count)])  50.1 us
    ppermute x16, starting transfers between devices, with_halo(): lax.ppermute(head, axis, [((i + 1) % count, i) for i in range(count)])  46.3 us
    unnamed x6, local copies, waits for them, and re-layouts  24.5 us
    ppermute x16, waiting for transfers between devices, with_halo(): lax.ppermute(head, axis, [((i + 1) % count, i) for i in range(count)])  7.54 us
    ppermute x16, starting transfers between devices, with_halo(): lax.ppermute(tail, axis, [(i, (i + 1) % count) for i in range(count)])  7.29 us
    all_to_all x1, starting transfers between devices, local(): lax.all_to_all(index_panels, 'col', split_axis=2, concat_axis=1, tiled=True)  7.28 us
    all_to_all x1, local copies, waits for them, and re-layouts, local(): lax.all_to_all(index_panels, 'col', split_axis=2, concat_axis=1, tiled=True)  6.41 us
    add x8, other arithmetic, slope(): diffraction * laplace(padded)  4.96 us
  transfers between devices with their start and end apart: 33, of which 22 were waited for; matrix products, arithmetic and copies ran while one was open for 1% of the time, Pallas kernels for 0%

commit v1 on v0

v1 whole, which is shorter than its diff:
```python
import functools

import jax
import jax.numpy as jnp
from jax import lax
from jax.experimental import pallas as pl
from jax.experimental.pallas import tpu as pltpu
from jax.sharding import PartitionSpec as P

STEPS = 2
MESH = pl.DeviceIdType.MESH
HALO = 16
PAD = 8
LANES = 128

diffraction = 0.15
phase_gain = 0.25
near = diffraction * 16.0 / 12.0
far = diffraction / 12.0
mid = diffraction * 60.0 / 12.0


def kernel(nr, nc, field, panels_in, out, panels, pack, planes, e, s1, s2, s3,
           strips, side, corners, load_sem, send_sem, plane_recv, fwd_send, fwd_recv,
           halo_send, halo_recv):
    n_planes, part, width = panels.shape
    _, rows, cols = out.shape
    wide = cols + LANES
    sub = HALO // part
    top = PAD + HALO
    last = n_planes - 1
    r, c = lax.axis_index("row"), lax.axis_index("col")
    up, down = lax.rem(r + nr - 1, nr), lax.rem(r + 1, nr)
    left, right = lax.rem(c + nc - 1, nc), lax.rem(c + 1, nc)

    load_field = pltpu.make_async_copy(field, e.at[:, pl.ds(top, rows), pl.ds(0, cols)], load_sem.at[0])
    load_field.start()
    load_panels = pltpu.make_async_copy(panels_in, panels, load_sem.at[1])
    load_panels.start()

    barrier = pltpu.get_barrier_semaphore()
    peers = [(r, lax.rem(c + k, nc)) for k in range(1, nc)]
    peers += [(y, x) for y in (up, down) for x in (left, c, right)]
    for peer in peers:
        pl.semaphore_signal(barrier, inc=1, device_id=peer, device_id_type=MESH)

    lane = lax.broadcasted_iota(jnp.int32, (part, LANES), 1)
    load_panels.wait()

    def pack_plane(p):
        for d in range(nc):
            pack[p, d, :, 0:cols] = panels[p, :, d * cols:(d + 1) * cols]
            if p < last:
                after = (d + 1) * cols % width
                before = (d * cols - LANES) % width
                pack[p, d, :, cols:wide] = jnp.where(
                    lane < LANES // 2,
                    panels[p, :, after:after + LANES].astype(jnp.float32),
                    panels[p, :, before:before + LANES].astype(jnp.float32),
                ).astype(pack.dtype)

    def plane_copy(p, k):
        to = lax.rem(c + k, nc)
        span = wide if p < last else cols
        return pltpu.make_async_remote_copy(
            src_ref=pack.at[p, to, :, pl.ds(0, span)],
            dst_ref=planes.at[p, sub + c, :, pl.ds(0, span)],
            send_sem=send_sem.at[p, k],
            recv_sem=plane_recv.at[p, k],
            device_id=(r, to),
            device_id_type=MESH,
        )

    def send_plane(p):
        for k in range(1, nc):
            plane_copy(p, k).start()
        planes[p, sub + c] = pack[p, c]

    pack_plane(0)
    load_field.wait()
    for i in range(2):
        strips[0, i] = e[i, top:top + rows, 0:LANES].T[0:HALO]
        strips[1, i] = e[i, top:top + rows, cols - LANES:cols].T[LANES - HALO:LANES]

    def remote(src, dst, at, to):
        return pltpu.make_async_remote_copy(
            src_ref=src, dst_ref=dst, send_sem=halo_send.at[at], recv_sem=halo_recv.at[at],
            device_id=to, device_id_type=MESH,
        )

    low, high = pl.ds(0, HALO), pl.ds(rows - HALO, HALO)
    first_tile, last_tile = pl.ds(0, LANES), pl.ds(cols - LANES, LANES)
    halos = [
        remote(field.at[:, high, :], e.at[:, pl.ds(PAD, HALO), pl.ds(0, cols)], 0, (down, c)),
        remote(field.at[:, low, :], e.at[:, pl.ds(top + rows, HALO), pl.ds(0, cols)], 1, (up, c)),
        remote(strips.at[0], side.at[:, pl.ds(0, HALO), :], 2, (r, left)),
        remote(strips.at[1], side.at[:, pl.ds(LANES - HALO, HALO), :], 3, (r, right)),
        remote(field.at[:, high, first_tile], corners.at[0], 4, (down, left)),
        remote(field.at[:, high, last_tile], corners.at[1], 5, (down, right)),
        remote(field.at[:, low, first_tile], corners.at[2], 6, (up, left)),
        remote(field.at[:, low, last_tile], corners.at[3], 7, (up, right)),
    ]

    pl.semaphore_wait(barrier, len(peers))
    for copy in halos:
        copy.start()
    send_plane(0)
    for p in range(1, n_planes):
        pack_plane(p)
        send_plane(p)

    for copy in halos:
        copy.wait()
    tile_lane = lax.broadcasted_iota(jnp.int32, (HALO, LANES), 1)
    for i in range(2):
        e[i, top:top + rows, cols:wide] = side[i].T
        e[i, PAD:top, cols:wide] = jnp.where(tile_lane < LANES // 2, corners[0, i], corners[1, i])
        e[i, top + rows:top + rows + HALO, cols:wide] = jnp.where(
            tile_lane < LANES // 2, corners[2, i], corners[3, i])

    def forwards(p):
        blocks = rows // part
        make = lambda src, dst, at, to: pltpu.make_async_remote_copy(
            src_ref=planes.at[p, pl.ds(src, sub)], dst_ref=planes.at[p, pl.ds(dst, sub)],
            send_sem=fwd_send.at[p, at], recv_sem=fwd_recv.at[p, at],
            device_id=(to, c), device_id_type=MESH,
        )
        return [make(blocks, 0, 0, down), make(sub, sub + blocks, 1, up)]

    def take_plane(p):
        for k in range(1, nc):
            plane_copy(p, k).wait_recv()
        if p < last:
            copies = forwards(p)
            for copy in copies:
                copy.start()
            for copy in copies:
                copy.wait()

    def evaluate(src, p, begin, end, finish):
        def block(b, carry):
            row = pl.multiple_of(b * HALO, HALO)
            if sub == 1:
                plane = planes[p, b].astype(jnp.float32)
            else:
                plane = jnp.concatenate(
                    [planes[p, b * sub + i].astype(jnp.float32) for i in range(sub)], axis=0)
            factor = phase_gain * plane - mid
            totals = []
            for i in range(2):
                window = src[i, pl.ds(row, HALO + 2 * PAD), :]
                tall = HALO + 2 * PAD
                centre = window[PAD:PAD + HALO]
                shift_y = lambda n: pltpu.roll(window, n % tall, 0)[PAD:PAD + HALO]
                shift_x = lambda n: pltpu.roll(centre, n % wide, 1)
                one = (shift_y(1) + shift_y(-1)) + (shift_x(1) + shift_x(-1))
                two = (shift_y(2) + shift_y(-2)) + (shift_x(2) + shift_x(-2))
                totals.append(near * one - far * two + factor * centre)
            finish(pl.ds(pl.multiple_of(row + PAD, PAD), HALO), b, (-totals[1], totals[0]))
            return carry

        lax.fori_loop(begin, end, block, 0)

    def stage(dst, weight):
        def finish(at, b, k):
            for i in range(2):
                dst[i, at, :] = e[i, at, :] + weight * k[i]
        return finish

    def close(at, b, k):
        for i in range(2):
            e[i, at, :] = (s1[i, at, :] + 2.0 * s2[i, at, :] + s3[i, at, :] - e[i, at, :]) * (1.0 / 3.0) + k[i] * (1.0 / 6.0)

    def close_out(at, b, k):
        here = pl.ds(pl.multiple_of((b - 1) * HALO, HALO), HALO)
        for i in range(2):
            value = (s1[i, at, :] + 2.0 * s2[i, at, :] + s3[i, at, :] - e[i, at, :]) * (1.0 / 3.0) + k[i] * (1.0 / 6.0)
            out[i, here, :] = value[:, 0:cols]

    full = rows // HALO + 2
    take_plane(0)
    for step in range(STEPS):
        p = 2 * step
        evaluate(e, p, 0, full, stage(s1, 0.5))
        take_plane(p + 1)
        evaluate(s1, p + 1, 0, full, stage(s2, 0.5))
        evaluate(s2, p + 1, 0, full, stage(s3, 1.0))
        take_plane(p + 2)
        if step < STEPS - 1:
            evaluate(s3, p + 2, 0, full, close)
        else:
            evaluate(s3, p + 2, 1, full - 1, close_out)

    for p in range(n_planes):
        for k in range(1, nc):
            plane_copy(p, k).wait_send()


def solution(mesh):
    nr, nc = mesh.shape["row"], mesh.shape["col"]

    def local(optical_field, index_panels):
        _, rows, cols = optical_field.shape
        n_planes, part, width = index_panels.shape
        wide = cols + LANES
        tall = rows + 2 * HALO + 2 * PAD
        grid = pltpu.VMEM((2, tall, wide), jnp.float32)
        return pl.pallas_call(
            functools.partial(kernel, nr, nc),
            out_shape=jax.ShapeDtypeStruct(optical_field.shape, jnp.float32),
            in_specs=[pl.BlockSpec(memory_space=pl.ANY)] * 2,
            out_specs=pl.BlockSpec(memory_space=pltpu.VMEM),
            scratch_shapes=[
                pltpu.VMEM((n_planes, part, width), jnp.bfloat16),
                pltpu.VMEM((n_planes, nc, part, wide), jnp.bfloat16),
                pltpu.VMEM((n_planes, (rows + 2 * HALO) // part, part, wide), jnp.bfloat16),
                grid, grid, grid, grid,
                pltpu.VMEM((2, 2, HALO, rows), jnp.float32),
                pltpu.VMEM((2, LANES, rows), jnp.float32),
                pltpu.VMEM((4, 2, HALO, LANES), jnp.float32),
                pltpu.SemaphoreType.DMA((2,)),
                pltpu.SemaphoreType.DMA((n_planes, nc)),
                pltpu.SemaphoreType.DMA((n_planes, nc)),
                pltpu.SemaphoreType.DMA((n_planes, 2)),
                pltpu.SemaphoreType.DMA((n_planes, 2)),
                pltpu.SemaphoreType.DMA((8,)),
                pltpu.SemaphoreType.DMA((8,)),
            ],
            compiler_params=pltpu.CompilerParams(
                collective_id=0, has_side_effects=True, vmem_limit_bytes=48 * 1024 * 1024),
        )(optical_field, index_panels)

    return jax.shard_map(
        local, mesh=mesh,
        in_specs=(P(None, "row", "col"), P(None, ("row", "col"), None)),
        out_specs=P(None, "row", "col"), check_vma=False,
    )
```

time: 163 us -> 42.7 us (0.26)
  the two profiles are of different devices: /device:TPU:0 before, /device:TPU:13 now
where the time goes in v1:
time: 42.7 us; the launch traced here: 42.5 us
  Pallas kernels  39.6 us (93%)
  local copies, waits for them, and re-layouts  2.92 us (7%)
    pallas_call x1, Pallas kernels, local(): pl.pallas_call(functools.partial(kernel, nr, nc), out_shape=jax.ShapeDtyp...  39.6 us
    unnamed x5, local copies, waits for them, and re-layouts  2.92 us

profile of v1, /device:TPU:13, one launch (start us, length us, event | category | flops | bytes accessed | tf_op | source)
XLA Modules:
  0.0 42.5 jit_solution(7469173869955331697)
XLA Ops:
  0.0 0.0 copy-start
  0.0 1.1 %copy-done = bf16[5,16,4096]{2,1,0:T(8,128)(2,1)S(1)} copy-done((bf16[5,16,4096]{2,1,0:T(8,128)(2,1)S(1)}, bf16[5,16,4096]{2,1,0:T(8,128)(2,1)}, u32[]{:S(2)}) %copy-start) | copy-done | bytes 655384
  1.1 0.0 copy-start.1
  1.1 1.0 %copy-done.1 = f32[2,128,512]{2,1,0:T(8,128)S(1)} copy-done((f32[2,128,512]{2,1,0:T(8,128)S(1)}, f32[2,128,512]{2,1,0:T(8,128)}, u32[]{:S(2)}) %copy-start.1) | copy-done | bytes 524312
  2.1 39.6 %shard_map.28 = f32[2,128,512]{2,1,0:T(8,128)S(1)} custom-call(f32[2,128,512]{2,1,0:T(8,128)S(1)} %copy-done.1, bf16[5,16,4096]{2,1,0:T(8,128)(2,1)S(1)} %copy-done), custom_call_target="tpu_custom_call" | custom-call | tf_op jit(solution)/shard_map/pallas_call | solution.py:208
  41.7 0.8 %copy.4 = f32[2,128,512]{2,1,0:T(8,128)} copy(f32[2,128,512]{2,1,0:T(8,128)S(1)} %shard_map.28) | data formatting | bytes 1048576
Async XLA Ops:
  0.0 1.1 %copy-start = (bf16[5,16,4096]{2,1,0:T(8,128)(2,1)S(1)}, bf16[5,16,4096]{2,1,0:T(8,128)(2,1)}, u32[]{:S(2)}) copy-start(bf16[5,16,4096]{2,1,0:T(8,128)(2,1)} %panels_in.1) | copy-start | bytes 1966084
  1.1 1.0 %copy-start.1 = (f32[2,128,512]{2,1,0:T(8,128)S(1)}, f32[2,128,512]{2,1,0:T(8,128)}, u32[]{:S(2)}) copy-start(f32[2,128,512]{2,1,0:T(8,128)} %field.1) | copy-start | bytes 1572868

commit v2 on v1

--- a/solution.py
+++ b/solution.py
@@ -20,23 +20,20 @@
 mid = diffraction * 60.0 / 12.0
 
 
-def kernel(nr, nc, field, panels_in, out, panels, pack, planes, e, s1, s2, s3,
-           strips, side, corners, load_sem, send_sem, plane_recv, fwd_send, fwd_recv,
+def kernel(nr, nc, ahead, field, panels_in, out, panels, pack, gathered, planes, edges, e, s1, s2, s3,
+           strips, side, corners, load_sem, send_sem, plane_recv, edge_send, edge_recv, fwd_send, fwd_recv,
            halo_send, halo_recv):
     n_planes, part, width = panels.shape
     _, rows, cols = out.shape
     wide = cols + LANES
     sub = HALO // part
+    blocks = rows // part
     top = PAD + HALO
     last = n_planes - 1
+    pair = 2 * HALO
     r, c = lax.axis_index("row"), lax.axis_index("col")
     up, down = lax.rem(r + nr - 1, nr), lax.rem(r + 1, nr)
     left, right = lax.rem(c + nc - 1, nc), lax.rem(c + 1, nc)
-
-    load_field = pltpu.make_async_copy(field, e.at[:, pl.ds(top, rows), pl.ds(0, cols)], load_sem.at[0])
-    load_field.start()
-    load_panels = pltpu.make_async_copy(panels_in, panels, load_sem.at[1])
-    load_panels.start()
 
     barrier = pltpu.get_barrier_semaphore()
     peers = [(r, lax.rem(c + k, nc)) for k in range(1, nc)]
@@ -44,43 +41,54 @@
     for peer in peers:
         pl.semaphore_signal(barrier, inc=1, device_id=peer, device_id_type=MESH)
 
+    load_field = pltpu.make_async_copy(field, e.at[:, pl.ds(top, rows), pl.ds(0, cols)], load_sem.at[0])
+    load_field.start()
+    load_panels = pltpu.make_async_copy(panels_in, panels, load_sem.at[1])
+    load_panels.start()
+    own_columns = pl.ds(pl.multiple_of(c * cols, LANES), cols)
+    own_planes = pltpu.make_async_copy(panels_in.at[:, :, own_columns], planes.at[:, sub + c], load_sem.at[2])
+    own_planes.start()
+
     lane = lax.broadcasted_iota(jnp.int32, (part, LANES), 1)
     load_panels.wait()
-
-    def pack_plane(p):
-        for d in range(nc):
-            pack[p, d, :, 0:cols] = panels[p, :, d * cols:(d + 1) * cols]
-            if p < last:
-                after = (d + 1) * cols % width
-                before = (d * cols - LANES) % width
-                pack[p, d, :, cols:wide] = jnp.where(
-                    lane < LANES // 2,
-                    panels[p, :, after:after + LANES].astype(jnp.float32),
-                    panels[p, :, before:before + LANES].astype(jnp.float32),
-                ).astype(pack.dtype)
-
-    def plane_copy(p, k):
-        to = lax.rem(c + k, nc)
-        span = wide if p < last else cols
-        return pltpu.make_async_remote_copy(
-            src_ref=pack.at[p, to, :, pl.ds(0, span)],
-            dst_ref=planes.at[p, sub + c, :, pl.ds(0, span)],
-            send_sem=send_sem.at[p, k],
-            recv_sem=plane_recv.at[p, k],
-            device_id=(r, to),
-            device_id_type=MESH,
-        )
-
-    def send_plane(p):
-        for k in range(1, nc):
-            plane_copy(p, k).start()
-        planes[p, sub + c] = pack[p, c]
-
-    pack_plane(0)
+    for d in range(nc):
+        after = (d + 1) * cols % width
+        before = (d * cols - LANES) % width
+        tile = jnp.zeros((part, LANES), jnp.float32)
+        for p in range(last):
+            at = pair * p
+            tile = jnp.where((lane >= at) & (lane < at + HALO), pltpu.roll(
+                panels[p, :, after:after + LANES].astype(jnp.float32), at, 1), tile)
+            at += HALO
+            tile = jnp.where((lane >= at) & (lane < at + HALO), pltpu.roll(
+                panels[p, :, before:before + LANES].astype(jnp.float32), (at + HALO) % LANES, 1), tile)
+        pack[d] = tile.astype(pack.dtype)
+
     load_field.wait()
     for i in range(2):
         strips[0, i] = e[i, top:top + rows, 0:LANES].T[0:HALO]
         strips[1, i] = e[i, top:top + rows, cols - LANES:cols].T[LANES - HALO:LANES]
+
+    def plane_copy(p, k):
+        to = lax.rem(c + k, nc)
+        return pltpu.make_async_remote_copy(
+            src_ref=panels_in.at[p, :, pl.ds(pl.multiple_of(to * cols, LANES), cols)],
+            dst_ref=planes.at[p, sub + c],
+            send_sem=send_sem.at[p, k], recv_sem=plane_recv.at[p, k],
+            device_id=(r, to), device_id_type=MESH,
+        )
+
+    def send_plane(p):
+        for k in range(1, nc):
+            plane_copy(p, k).start()
+
+    def edge_copy(k):
+        to = lax.rem(c + k, nc)
+        return pltpu.make_async_remote_copy(
+            src_ref=pack.at[to], dst_ref=gathered.at[sub + c],
+            send_sem=edge_send.at[k], recv_sem=edge_recv.at[k],
+            device_id=(r, to), device_id_type=MESH,
+        )
 
     def remote(src, dst, at, to):
         return pltpu.make_async_remote_copy(
@@ -102,12 +110,27 @@
     ]
 
     pl.semaphore_wait(barrier, len(peers))
+    for k in range(1, nc):
+        edge_copy(k).start()
     for copy in halos:
         copy.start()
-    send_plane(0)
-    for p in range(1, n_planes):
-        pack_plane(p)
+    for p in range(ahead):
         send_plane(p)
+    gathered[sub + c] = pack[c]
+
+    def forwards(ref, at):
+        make = lambda src, dst, which, to: pltpu.make_async_remote_copy(
+            src_ref=ref.at[pl.ds(src, sub)], dst_ref=ref.at[pl.ds(dst, sub)],
+            send_sem=fwd_send.at[at, which], recv_sem=fwd_recv.at[at, which],
+            device_id=(to, c), device_id_type=MESH,
+        )
+        return [make(blocks, 0, 0, down), make(sub, sub + blocks, 1, up)]
+
+    for k in range(1, nc):
+        edge_copy(k).wait_recv()
+    edge_forwards = forwards(gathered, last)
+    for copy in edge_forwards:
+        copy.start()
 
     for copy in halos:
         copy.wait()
@@ -118,33 +141,38 @@
         e[i, top + rows:top + rows + HALO, cols:wide] = jnp.where(
             tile_lane < LANES // 2, corners[2, i], corners[3, i])
 
-    def forwards(p):
-        blocks = rows // part
-        make = lambda src, dst, at, to: pltpu.make_async_remote_copy(
-            src_ref=planes.at[p, pl.ds(src, sub)], dst_ref=planes.at[p, pl.ds(dst, sub)],
-            send_sem=fwd_send.at[p, at], recv_sem=fwd_recv.at[p, at],
-            device_id=(to, c), device_id_type=MESH,
-        )
-        return [make(blocks, 0, 0, down), make(sub, sub + blocks, 1, up)]
+    for copy in edge_forwards:
+        copy.wait()
+    for b in range(blocks + 2 * sub):
+        tile = gathered[b].astype(jnp.float32)
+        for p in range(last):
+            edges[p, b] = jnp.where(
+                lane < LANES // 2,
+                pltpu.roll(tile, (LANES - pair * p) % LANES, 1),
+                pltpu.roll(tile, (LANES - pair * (p + 1)) % LANES, 1),
+            ).astype(edges.dtype)
+    own_planes.wait()
 
     def take_plane(p):
         for k in range(1, nc):
             plane_copy(p, k).wait_recv()
-        if p < last:
-            copies = forwards(p)
-            for copy in copies:
-                copy.start()
-            for copy in copies:
-                copy.wait()
+        copies = forwards(planes.at[p], p) if p < last else []
+        for copy in copies:
+            copy.start()
+        if p + ahead < n_planes:
+            send_plane(p + ahead)
+        for copy in copies:
+            copy.wait()
 
     def evaluate(src, p, begin, end, finish):
         def block(b, carry):
             row = pl.multiple_of(b * HALO, HALO)
-            if sub == 1:
-                plane = planes[p, b].astype(jnp.float32)
-            else:
-                plane = jnp.concatenate(
-                    [planes[p, b * sub + i].astype(jnp.float32) for i in range(sub)], axis=0)
+            pieces = []
+            for i in range(sub):
+                piece = planes[p, b * sub + i].astype(jnp.float32)
+                edge = edges[min(p, last - 1), b * sub + i].astype(jnp.float32)
+                pieces.append(jnp.concatenate([piece, edge], axis=1))
+            plane = pieces[0] if sub == 1 else jnp.concatenate(pieces, axis=0)
             factor = phase_gain * plane - mid
             totals = []
             for i in range(2):
@@ -159,7 +187,7 @@
             finish(pl.ds(pl.multiple_of(row + PAD, PAD), HALO), b, (-totals[1], totals[0]))
             return carry
 
-        lax.fori_loop(begin, end, block, 0)
+        lax.fori_loop(begin, end, block, 0, unroll=end - begin)
 
     def stage(dst, weight):
         def finish(at, b, k):
@@ -191,8 +219,9 @@
         else:
             evaluate(s3, p + 2, 1, full - 1, close_out)
 
-    for p in range(n_planes):
-        for k in range(1, nc):
+    for k in range(1, nc):
+        edge_copy(k).wait_send()
+        for p in range(n_planes):
             plane_copy(p, k).wait_send()
 
 
@@ -203,31 +232,36 @@
         _, rows, cols = optical_field.shape
         n_planes, part, width = index_panels.shape
         wide = cols + LANES
+        count = (rows + 2 * HALO) // part
         tall = rows + 2 * HALO + 2 * PAD
         grid = pltpu.VMEM((2, tall, wide), jnp.float32)
         return pl.pallas_call(
-            functools.partial(kernel, nr, nc),
+            functools.partial(kernel, nr, nc, 2),
             out_shape=jax.ShapeDtypeStruct(optical_field.shape, jnp.float32),
-            in_specs=[pl.BlockSpec(memory_space=pl.ANY)] * 2,
+            in_specs=[pl.BlockSpec(memory_space=pltpu.HBM)] * 2,
             out_specs=pl.BlockSpec(memory_space=pltpu.VMEM),
             scratch_shapes=[
                 pltpu.VMEM((n_planes, part, width), jnp.bfloat16),
-                pltpu.VMEM((n_planes, nc, part, wide), jnp.bfloat16),
-                pltpu.VMEM((n_planes, (rows + 2 * HALO) // part, part, wide), jnp.bfloat16),
+                pltpu.VMEM((nc, part, LANES), jnp.bfloat16),
+                pltpu.VMEM((count, part, LANES), jnp.bfloat16),
+                pltpu.VMEM((n_planes, count, part, cols), jnp.bfloat16),
+                pltpu.VMEM((n_planes - 1, count, part, LANES), jnp.bfloat16),
                 grid, grid, grid, grid,
                 pltpu.VMEM((2, 2, HALO, rows), jnp.float32),
                 pltpu.VMEM((2, LANES, rows), jnp.float32),
                 pltpu.VMEM((4, 2, HALO, LANES), jnp.float32),
-                pltpu.SemaphoreType.DMA((2,)),
+                pltpu.SemaphoreType.DMA((3,)),
                 pltpu.SemaphoreType.DMA((n_planes, nc)),
                 pltpu.SemaphoreType.DMA((n_planes, nc)),
+                pltpu.SemaphoreType.DMA((nc,)),
+                pltpu.SemaphoreType.DMA((nc,)),
                 pltpu.SemaphoreType.DMA((n_planes, 2)),
                 pltpu.SemaphoreType.DMA((n_planes, 2)),
                 pltpu.SemaphoreType.DMA((8,)),
                 pltpu.SemaphoreType.DMA((8,)),
             ],
             compiler_params=pltpu.CompilerParams(
-                collective_id=0, has_side_effects=True, vmem_limit_bytes=48 * 1024 * 1024),
+                collective_id=0, has_side_effects=True, vmem_limit_bytes=63 * 1024 * 1024),
         )(optical_field, index_panels)
 
     return jax.shard_map(

time: 42.7 us -> 33 us (0.77)
  the two profiles are of different devices: /device:TPU:13 before, /device:TPU:0 now
where the time goes in v2:
time: 33 us; the launch traced here: 32.8 us
  Pallas kernels  30.9 us (94%)
  local copies, waits for them, and re-layouts  1.87 us (6%)
    pallas_call x1, Pallas kernels, local(): pl.pallas_call(functools.partial(kernel, nr, nc, 2), out_shape=jax.ShapeD...  30.9 us
    unnamed x1, local copies, waits for them, and re-layouts  1.87 us

profile of v2, /device:TPU:0, one launch (start us, length us, event | category | flops | bytes accessed | tf_op | source)
XLA Modules:
  0.0 32.8 jit_solution(6318369849686379614)
XLA Ops:
  0.0 30.9 %shard_map.28 = f32[2,128,512]{2,1,0:T(8,128)} custom-call(f32[2,128,512]{2,1,0:T(8,128)} %field.1, bf16[5,16,4096]{2,1,0:T(8,128)(2,1)} %panels_in.1), custom_call_target="tpu_custom_call" | custom-call | tf_op jit(solution)/shard_map/pallas_call | solution.py:238
  30.9 1.9 %copy.4 = f32[2,128,512]{2,1,0:T(8,128)} copy(f32[2,128,512]{2,1,0:T(8,128)} %shard_map.28) | data formatting | bytes 1048576

commit v3 on v2

--- a/solution.py
+++ b/solution.py
@@ -49,6 +49,58 @@
     own_planes = pltpu.make_async_copy(panels_in.at[:, :, own_columns], planes.at[:, sub + c], load_sem.at[2])
     own_planes.start()
 
+    def plane_copy(p, k):
+        to = lax.rem(c + k, nc)
+        return pltpu.make_async_remote_copy(
+            src_ref=panels_in.at[p, :, pl.ds(pl.multiple_of(to * cols, LANES), cols)],
+            dst_ref=planes.at[p, sub + c],
+            send_sem=send_sem.at[p, k], recv_sem=plane_recv.at[p, k],
+            device_id=(r, to), device_id_type=MESH,
+        )
+
+    def send_plane(p):
+        for k in range(1, nc):
+            plane_copy(p, k).start()
+
+    def edge_copy(k):
+        to = lax.rem(c + k, nc)
+        return pltpu.make_async_remote_copy(
+            src_ref=pack.at[to], dst_ref=gathered.at[sub + c],
+            send_sem=edge_send.at[k], recv_sem=edge_recv.at[k],
+            device_id=(r, to), device_id_type=MESH,
+        )
+
+    def remote(src, dst, at, to):
+        return pltpu.make_async_remote_copy(
+            src_ref=src, dst_ref=dst, send_sem=halo_send.at[at], recv_sem=halo_recv.at[at],
+            device_id=to, device_id_type=MESH,
+        )
+
+    low, high = pl.ds(0, HALO), pl.ds(rows - HALO, HALO)
+    first_tile, last_tile = pl.ds(0, LANES), pl.ds(cols - LANES, LANES)
+    halos = [
+        remote(field.at[:, high, :], e.at[:, pl.ds(PAD, HALO), pl.ds(0, cols)], 0, (down, c)),
+        remote(field.at[:, low, :], e.at[:, pl.ds(top + rows, HALO), pl.ds(0, cols)], 1, (up, c)),
+        remote(strips.at[0], side.at[:, pl.ds(0, HALO), :], 2, (r, left)),
+        remote(strips.at[1], side.at[:, pl.ds(LANES - HALO, HALO), :], 3, (r, right)),
+        remote(field.at[:, high, first_tile], corners.at[0], 4, (down, left)),
+        remote(field.at[:, high, last_tile], corners.at[1], 5, (down, right)),
+        remote(field.at[:, low, first_tile], corners.at[2], 6, (up, left)),
+        remote(field.at[:, low, last_tile], corners.at[3], 7, (up, right)),
+    ]
+
+    pl.semaphore_wait(barrier, len(peers))
+    for copy in halos[:2] + halos[4:]:
+        copy.start()
+    send_plane(0)
+    load_field.wait()
+    for i in range(2):
+        strips[0, i] = e[i, top:top + rows, 0:LANES].T[0:HALO]
+        strips[1, i] = e[i, top:top + rows, cols - LANES:cols].T[LANES - HALO:LANES]
+
+    for copy in halos[2:4]:
+        copy.start()
+
     lane = lax.broadcasted_iota(jnp.int32, (part, LANES), 1)
     load_panels.wait()
     for d in range(nc):
@@ -64,57 +116,9 @@
                 panels[p, :, before:before + LANES].astype(jnp.float32), (at + HALO) % LANES, 1), tile)
         pack[d] = tile.astype(pack.dtype)
 
-    load_field.wait()
-    for i in range(2):
-        strips[0, i] = e[i, top:top + rows, 0:LANES].T[0:HALO]
-        strips[1, i] = e[i, top:top + rows, cols - LANES:cols].T[LANES - HALO:LANES]
-
-    def plane_copy(p, k):
-        to = lax.rem(c + k, nc)
-        return pltpu.make_async_remote_copy(
-            src_ref=panels_in.at[p, :, pl.ds(pl.multiple_of(to * cols, LANES), cols)],
-            dst_ref=planes.at[p, sub + c],
-            send_sem=send_sem.at[p, k], recv_sem=plane_recv.at[p, k],
-            device_id=(r, to), device_id_type=MESH,
-        )
-
-    def send_plane(p):
-        for k in range(1, nc):
-            plane_copy(p, k).start()
-
-    def edge_copy(k):
-        to = lax.rem(c + k, nc)
-        return pltpu.make_async_remote_copy(
-            src_ref=pack.at[to], dst_ref=gathered.at[sub + c],
-            send_sem=edge_send.at[k], recv_sem=edge_recv.at[k],
-            device_id=(r, to), device_id_type=MESH,
-        )
-
-    def remote(src, dst, at, to):
-        return pltpu.make_async_remote_copy(
-            src_ref=src, dst_ref=dst, send_sem=halo_send.at[at], recv_sem=halo_recv.at[at],
-            device_id=to, device_id_type=MESH,
-        )
-
-    low, high = pl.ds(0, HALO), pl.ds(rows - HALO, HALO)
-    first_tile, last_tile = pl.ds(0, LANES), pl.ds(cols - LANES, LANES)
-    halos = [
-        remote(field.at[:, high, :], e.at[:, pl.ds(PAD, HALO), pl.ds(0, cols)], 0, (down, c)),
-        remote(field.at[:, low, :], e.at[:, pl.ds(top + rows, HALO), pl.ds(0, cols)], 1, (up, c)),
-        remote(strips.at[0], side.at[:, pl.ds(0, HALO), :], 2, (r, left)),
-        remote(strips.at[1], side.at[:, pl.ds(LANES - HALO, HALO), :], 3, (r, right)),
-        remote(field.at[:, high, first_tile], corners.at[0], 4, (down, left)),
-        remote(field.at[:, high, last_tile], corners.at[1], 5, (down, right)),
-        remote(field.at[:, low, first_tile], corners.at[2], 6, (up, left)),
-        remote(field.at[:, low, last_tile], corners.at[3], 7, (up, right)),
-    ]
-
-    pl.semaphore_wait(barrier, len(peers))
     for k in range(1, nc):
         edge_copy(k).start()
-    for copy in halos:
-        copy.start()
-    for p in range(ahead):
+    for p in range(1, ahead):
         send_plane(p)
     gathered[sub + c] = pack[c]
 
@@ -161,11 +165,11 @@
             copy.start()
         if p + ahead < n_planes:
             send_plane(p + ahead)
-        for copy in copies:
-            copy.wait()
-
-    def evaluate(src, p, begin, end, finish):
-        def block(b, carry):
+        return copies
+
+    def evaluate(src, p, begin, end, finish, stride=1):
+        def block(n, carry):
+            b = n * stride
             row = pl.multiple_of(b * HALO, HALO)
             pieces = []
             for i in range(sub):
@@ -206,17 +210,26 @@
             out[i, here, :] = value[:, 0:cols]
 
     full = rows // HALO + 2
-    take_plane(0)
+
+    def first_evaluate(src, p, finish):
+        copies = take_plane(p)
+        evaluate(src, p, 1, full - 1, finish)
+        for copy in copies:
+            copy.wait()
+        evaluate(src, p, 0, 2, finish, full - 1)
+
     for step in range(STEPS):
         p = 2 * step
-        evaluate(e, p, 0, full, stage(s1, 0.5))
-        take_plane(p + 1)
-        evaluate(s1, p + 1, 0, full, stage(s2, 0.5))
+        if step == 0:
+            first_evaluate(e, p, stage(s1, 0.5))
+        else:
+            evaluate(e, p, 0, full, stage(s1, 0.5))
+        first_evaluate(s1, p + 1, stage(s2, 0.5))
         evaluate(s2, p + 1, 0, full, stage(s3, 1.0))
-        take_plane(p + 2)
         if step < STEPS - 1:
-            evaluate(s3, p + 2, 0, full, close)
+            first_evaluate(s3, p + 2, close)
         else:
+            take_plane(p + 2)
             evaluate(s3, p + 2, 1, full - 1, close_out)
 
     for k in range(1, nc):

time: 33 us -> 34.2 us (1.036)
  Pallas kernels: 30.9 us -> 32 us
    pallas_call x1, Pallas kernels: 30.9 us -> 32 us  [local(): pl.pallas_call(functools.partial(kernel, nr, nc, 2), out_shape=jax.ShapeD...]
where the time goes in v3:
time: 34.2 us; the launch traced here: 33.9 us
  Pallas kernels  32 us (94%)
  local copies, waits for them, and re-layouts  1.87 us (5%)
    pallas_call x1, Pallas kernels, local(): pl.pallas_call(functools.partial(kernel, nr, nc, 2), out_shape=jax.ShapeD...  32 us
    unnamed x1, local copies, waits for them, and re-layouts  1.87 us

profile of v3, /device:TPU:0, one launch (start us, length us, event | category | flops | bytes accessed | tf_op | source)
XLA Modules:
  0.0 33.9 jit_solution(9360198800173833344)
XLA Ops:
  0.0 32.0 %shard_map.28 = f32[2,128,512]{2,1,0:T(8,128)} custom-call(f32[2,128,512]{2,1,0:T(8,128)} %field.1, bf16[5,16,4096]{2,1,0:T(8,128)(2,1)} %panels_in.1), custom_call_target="tpu_custom_call" | custom-call | tf_op jit(solution)/shard_map/pallas_call | solution.py:251
  32.0 1.9 %copy.4 = f32[2,128,512]{2,1,0:T(8,128)} copy(f32[2,128,512]{2,1,0:T(8,128)} %shard_map.28) | data formatting | bytes 1048576

commit v4 on v3

--- a/solution.py
+++ b/solution.py
@@ -89,18 +89,6 @@
         remote(field.at[:, low, last_tile], corners.at[3], 7, (up, right)),
     ]
 
-    pl.semaphore_wait(barrier, len(peers))
-    for copy in halos[:2] + halos[4:]:
-        copy.start()
-    send_plane(0)
-    load_field.wait()
-    for i in range(2):
-        strips[0, i] = e[i, top:top + rows, 0:LANES].T[0:HALO]
-        strips[1, i] = e[i, top:top + rows, cols - LANES:cols].T[LANES - HALO:LANES]
-
-    for copy in halos[2:4]:
-        copy.start()
-
     lane = lax.broadcasted_iota(jnp.int32, (part, LANES), 1)
     load_panels.wait()
     for d in range(nc):
@@ -116,9 +104,17 @@
                 panels[p, :, before:before + LANES].astype(jnp.float32), (at + HALO) % LANES, 1), tile)
         pack[d] = tile.astype(pack.dtype)
 
+    load_field.wait()
+    for i in range(2):
+        strips[0, i] = e[i, top:top + rows, 0:LANES].T[0:HALO]
+        strips[1, i] = e[i, top:top + rows, cols - LANES:cols].T[LANES - HALO:LANES]
+
+    pl.semaphore_wait(barrier, len(peers))
     for k in range(1, nc):
         edge_copy(k).start()
-    for p in range(1, ahead):
+    for copy in halos:
+        copy.start()
+    for p in range(ahead):
         send_plane(p)
     gathered[sub + c] = pack[c]
 

time: 34.2 us -> 30.3 us (0.89)
  Pallas kernels: 32 us -> 28.1 us
    pallas_call x1, Pallas kernels: 32 us -> 28.1 us  [local(): pl.pallas_call(functools.partial(kernel, nr, nc, 2), out_shape=jax.ShapeD...]
where the time goes in v4:
time: 30.3 us; the launch traced here: 30 us
  Pallas kernels  28.1 us (93%)
  local copies, waits for them, and re-layouts  1.87 us (6%)
    pallas_call x1, Pallas kernels, local(): pl.pallas_call(functools.partial(kernel, nr, nc, 2), out_shape=jax.ShapeD...  28.1 us
    unnamed x1, local copies, waits for them, and re-layouts  1.87 us

profile of v4, /device:TPU:0, one launch (start us, length us, event | category | flops | bytes accessed | tf_op | source)
XLA Modules:
  0.0 30.0 jit_solution(4282116212710483003)
XLA Ops:
  0.0 28.1 %shard_map.28 = f32[2,128,512]{2,1,0:T(8,128)} custom-call(f32[2,128,512]{2,1,0:T(8,128)} %field.1, bf16[5,16,4096]{2,1,0:T(8,128)(2,1)} %panels_in.1), custom_call_target="tpu_custom_call" | custom-call | tf_op jit(solution)/shard_map/pallas_call | solution.py:247
  28.1 1.9 %copy.4 = f32[2,128,512]{2,1,0:T(8,128)} copy(f32[2,128,512]{2,1,0:T(8,128)} %shard_map.28) | data formatting | bytes 1048576
